TPU v7x, 32 devices: a whole 2x2x4 slice. The times are simulated.
32 devices in a mesh: grp: 8 (over z, y), chan: 4 (over x, core).
Axes of the slice: x: 2, y: 2, z: 4, core: 2. Of those that a mesh axis runs over, the one named last changes fastest.
Arguments:
- grad_out: bfloat16 [64, 8, 16, 128], P('grp', 'chan'), may hold values from -6 to 6
- feat_full: bfloat16 [64, 8, 16, 128], P('grp', 'chan'), may hold values from -6 to 6
- filters_full: bfloat16 [3, 3, 3, 128, 128], replicated, may hold values from -0.109375 to 0.109375
- upsample_weight: bfloat16 [2, 2, 2, 512, 128], replicated, may hold values from -0.1875 to 0.1875
- filters_half: bfloat16 [3, 3, 3, 512, 512], P(None, None, None, None, 'chan'), may hold values from -0.0546875 to 0.0546875
Outputs:
- grad_half: bfloat16 [4, 32, 8, 512], P('chan', 'grp')
- taps_grad: float32 [3, 3, 3, 128, 128], P(None, None, None, 'grp', 'chan')
All inputs are finite; a program needn't handle non-finite values.
Results may differ from a plain program's by a relative error of at most 0.0058.
Values may be sent and summed in bfloat16 or wider, within the bound.
No kernel may reach another device: no remote copies, remote signals or barrier semaphores. Data moves between devices by JAX's collectives and lax.ppermute only.
A program may use at most 64 MiB of HBM per device.

v0:
```python
import jax
import jax.numpy as jnp
from jax import lax
from jax.sharding import PartitionSpec as P


def padded_2(cells, sides, width):
    for axis, dim in sides:
        count = lax.axis_size(axis)
        ends = count - 1
        head = lax.slice_in_dim(cells, 0, width, axis=dim)
        tail = lax.slice_in_dim(cells, cells.shape[dim] - width, cells.shape[dim], axis=dim)
        cells = jnp.concatenate(
            [
                lax.ppermute(tail, axis, [(i, (i + 1) % count) for i in range(ends)]),
                cells,
                lax.ppermute(head, axis, [((i + 1) % count, i) for i in range(ends)]),
            ],
            axis=dim,
        )
    return cells


def spread_taps(padded, weight, extent, summed, swapped):
    for p in range(3):
        for q in range(3):
            for r in range(3):
                window = padded[
                    2 - p : 2 - p + extent[0], 2 - q : 2 - q + extent[1], 2 - r : 2 - r + extent[2]
                ]
                kernel = weight[q, p, r] if swapped else weight[p, q, r]
                summed = summed + jnp.einsum(
                    "xyzo,io->xyzi", window, kernel, preferred_element_type=jnp.float32
                )
    return summed


def body(grad_out, feat_full, filters_full, upsample_weight, filters_half):
    extent = grad_out.shape[:3]
    channels = grad_out.shape[3]
    stacked = jnp.stack([grad_out, feat_full])
    bordered = padded_2(stacked, (("grp", 1), ("chan", 2)), 1)
    bordered = jnp.pad(bordered, ((0, 0), (0, 0), (0, 0), (1, 1), (0, 0)))
    zeroed = jnp.zeros(extent + (channels,), jnp.float32)
    input_grad = spread_taps(bordered[0], filters_full, extent, zeroed, False).astype(jnp.bfloat16)
    features = bordered[1]
    tap_list = []
    for p in range(3):
        for q in range(3):
            for r in range(3):
                window = features[p : p + extent[0], q : q + extent[1], r : r + extent[2]]
                tap_list.append(
                    jnp.einsum(
                        "xyzi,xyzo->io", window, grad_out, preferred_element_type=jnp.float32
                    )
                )
    partial_taps = jnp.stack(tap_list).reshape(3, 3, 3, channels, channels)
    across = lax.psum_scatter(partial_taps, "grp", scatter_dimension=3, tiled=True)
    taps_grad = lax.psum_scatter(across, "chan", scatter_dimension=4, tiled=True)
    halves = input_grad.reshape(extent[0] // 2, 2, extent[1] // 2, 2, extent[2] // 2, 2, channels)
    coarse = jnp.einsum(
        "iajbkcd,abced->jike", halves, upsample_weight, preferred_element_type=jnp.float32
    ).astype(jnp.bfloat16)
    coarse_extent = coarse.shape[:3]
    wide = filters_half.shape[3]
    slab = lax.all_to_all(coarse, "chan", split_axis=3, concat_axis=0, tiled=True)
    slab = padded_2(slab, (("grp", 1),), 1)
    slab = jnp.pad(slab, ((1, 1), (0, 0), (1, 1), (0, 0)))
    count = lax.axis_size("chan") * coarse_extent[0]
    blank = jnp.zeros((count, coarse_extent[1], coarse_extent[2], wide), jnp.float32)
    result = lax.psum_scatter(
        spread_taps(slab, filters_half, (count, coarse_extent[1], coarse_extent[2]), blank, True),
        "chan",
        scatter_dimension=0,
        tiled=True,
    )
    grad_half = result.astype(jnp.bfloat16)
    return (grad_half, taps_grad)


def solution(mesh):
    in_specs = (
        P("grp", "chan", None, None),
        P("grp", "chan", None, None),
        P(),
        P(),
        P(None, None, None, None, "chan"),
    )
    out_specs = (P("chan", "grp", None, None), P(None, None, None, "grp", "chan"))
    return jax.shard_map(body, mesh=mesh, in_specs=in_specs, out_specs=out_specs, check_vma=False)
```

profile of v0, /device:TPU:0, one launch (start us, length us, event | category | flops | bytes accessed | tf_op | source)
XLA Modules:
  0.0 166.8 jit_solution(15116668181056318444)
XLA Ops:
  7.2 0.9 pad_maximum_fusion.2
  8.1 4.9 %collective-permute-start = (bf16[2,1,2,16,128]{4,3,2,1,0:T(8,128)(2,1)S(1)}, bf16[2,1,2,16,128]{4,3,2,1,0:T(8,128)(2,1)S(1)}, u32[]{:S(2)}, u32[]{:S(2)}) collective-permute-start(bf16[2,1,2,16,128]{4,3,2,1,0:T(8,128)(2,1)S(1)} %get-tuple-element.6), channel_id=1, source_target_pairs={{0,4},{4,8},{8,12},{12,16},{16,20},{20,24},{24,28},{1,5},{5,9},{9,... | collective-permute-start | bytes 49160 | tf_op jit(solution)/shard_map/ppermute | solution.py:15
  13.0 1.3 collective-permute-start.1
  14.4 4.2 %collective-permute-done.1 = bf16[2,1,2,16,128]{4,3,2,1,0:T(8,128)(2,1)S(1)} collective-permute-done((bf16[2,1,2,16,128]{4,3,2,1,0:T(8,128)(2,1)S(1)}, bf16[2,1,2,16,128]{4,3,2,1,0:T(8,128)(2,1)S(1)}, u32[]{:S(2)}, u32[]{:S(2)}) %collective-permute-start.1) | collective-permute-done | bytes 16416 | tf_op jit(solution)/shard_map/ppermute | solution.py:17
  18.6 0.9 pad_maximum_fusion
  19.5 1.3 collective-permute-start.2
  20.8 1.3 collective-permute-start.3
  22.1 3.6 %collective-permute-done.3 = bf16[2,10,1,16,128]{4,3,2,1,0:T(8,128)(2,1)S(1)} collective-permute-done((bf16[2,10,1,16,128]{4,3,2,1,0:T(8,128)(2,1)S(1)}, bf16[2,10,1,16,128]{4,3,2,1,0:T(8,128)(2,1)S(1)}, u32[]{:S(2)}, u32[]{:S(2)}) %collective-permute-start.3) | collective-permute-done | bytes 81952 | tf_op jit(solution)/shard_map/ppermute | solution.py:17
  25.7 1.1 select_maximum_fusion
  32.2 1.1 reshape.101
  33.3 4.4 %all-to-all-start = ((bf16[4,2,2048]{2,1,0:T(2,128)(2,1)}), bf16[4,2,2048]{2,1,0:T(2,128)(2,1)S(1)}, u32[]{:S(2)}, u32[]{:S(2)}) async-start(bf16[4,2,2048]{2,1,0:T(2,128)(2,1)} %reshape.101), calls=%async_computation | async-start | bytes 65536 | tf_op jit(solution)/shard_map/all_to_all | solution.py:66
  43.2 1.2 copy-done.2
  45.4 4.3 %collective-permute-start.4 = (bf16[4,1,8,128]{3,2,1,0:T(8,128)(2,1)S(1)}, bf16[4,1,8,128]{3,2,1,0:T(8,128)(2,1)S(1)}, u32[]{:S(2)}, u32[]{:S(2)}) collective-permute-start(bf16[4,1,8,128]{3,2,1,0:T(8,128)(2,1)S(1)} %get-tuple-element.8), channel_id=1, source_target_pairs={{0,4},{4,8},{8,12},{12,16},{16,20},{20,24},{24,28},{1,5},{5,9},{9,... | collective-permute-start | bytes 24584 | tf_op jit(solution)/shard_map/ppermute | solution.py:15
  49.7 1.6 collective-permute-start.5
  51.3 1.1 fusion.71
  52.4 3.1 %collective-permute-done.5 = bf16[4,1,8,128]{3,2,1,0:T(8,128)(2,1)S(1)} collective-permute-done((bf16[4,1,8,128]{3,2,1,0:T(8,128)(2,1)S(1)}, bf16[4,1,8,128]{3,2,1,0:T(8,128)(2,1)S(1)}, u32[]{:S(2)}, u32[]{:S(2)}) %collective-permute-start.5) | collective-permute-done | bytes 8224 | tf_op jit(solution)/shard_map/ppermute | solution.py:17
  55.6 1.1 fusion.59
  56.7 1.1 fusion.61
  57.8 1.1 fusion.63
  58.9 1.1 fusion.65
  60.0 1.1 fusion.69
  61.1 1.1 fusion.73
  62.2 1.1 fusion.87
  66.9 0.9 convolution_add_fusion.2
  67.9 46.4 %reduce-scatter.8.cloned.1.call-done = f32[3,3,3,16,128]{4,3,2,1,0:T(8,128)} async-done(((f32[3,3,3,128,128]{4,3,2,1,0:T(8,128)}), f32[3,3,3,16,128]{4,3,2,1,0:T(8,128)}) %reduce-scatter.8.cloned.1.call-update) | async-done | bytes 221200 | tf_op jit(solution)/shard_map/reduce_scatter | solution.py:58
  114.3 2.5 %copy.99 = f32[3,3,3,16,128]{3,2,1,0,4:T(4,128)S(1)} copy(f32[3,3,3,16,128]{4,3,2,1,0:T(8,128)} %reduce-scatter.8.cloned.1.call-done) | data formatting | bytes 442368
  116.8 1.7 %reshape.99 = f32[128,432]{1,0:T(8,128)} reshape(f32[128,3,3,3,16]{4,3,2,1,0:T(4,128)S(1)} %bitcast.656) | data formatting | bytes 442368
  118.5 17.2 %reduce-scatter.6.cloned.1.call-done = f32[1,4,8,512]{3,2,1,0:T(8,128)} async-done(((f32[4,4,8,512]{3,2,1,0:T(8,128)}), f32[1,4,8,512]{3,2,1,0:T(8,128)}) %reduce-scatter.6.cloned.1.call-update) | async-done | bytes 65552 | tf_op jit(solution)/shard_map/reduce_scatter | solution.py:71
  135.7 1.5 convert_element_type.27
  137.2 21.1 %reduce-scatter.10.cloned.1.call-done = f32[32,432]{1,0:T(8,128)} async-done(((f32[128,432]{1,0:T(8,128)}), f32[32,432]{1,0:T(8,128)}) %reduce-scatter.10.cloned.1.call-update) | async-done | bytes 55312
  158.3 1.1 reshape.100
  159.4 0.9 copy.100
  (99 shorter events, 15.2 us)
Async XLA Ops:
  7.2 24.3 %copy-start = (bf16[2,2,2,512,128]{4,3,2,1,0:T(8,128)(2,1)S(1)}, bf16[2,2,2,512,128]{4,3,2,1,0:T(8,128)(2,1)}, u32[]{:S(2)}) copy-start(bf16[2,2,2,512,128]{4,3,2,1,0:T(8,128)(2,1)} %param.8) | copy-start | bytes 3145732
  7.2 19.7 %copy-start.3 = (bf16[3,3,3,128,128]{4,3,2,1,0:T(8,128)(2,1)S(1)}, bf16[3,3,3,128,128]{4,3,2,1,0:T(8,128)(2,1)}, u32[]{:S(2)}) copy-start(bf16[3,3,3,128,128]{4,3,2,1,0:T(8,128)(2,1)} %param.7) | copy-start | bytes 2654212
  8.1 6.3 %collective-permute-start = (bf16[2,1,2,16,128]{4,3,2,1,0:T(8,128)(2,1)S(1)}, bf16[2,1,2,16,128]{4,3,2,1,0:T(8,128)(2,1)S(1)}, u32[]{:S(2)}, u32[]{:S(2)}) collective-permute-start(bf16[2,1,2,16,128]{4,3,2,1,0:T(8,128)(2,1)S(1)} %get-tuple-element.6), channel_id=1, source_target_pairs={{0,4},{4,8},{8,12},{12,16},{16,20},{20,24},{24,28},{1,5},{5,9},{9,... | collective-permute-start | bytes 49160 | tf_op jit(solution)/shard_map/ppermute | solution.py:15
  13.0 5.6 %collective-permute-start.1 = (bf16[2,1,2,16,128]{4,3,2,1,0:T(8,128)(2,1)S(1)}, bf16[2,1,2,16,128]{4,3,2,1,0:T(8,128)(2,1)S(1)}, u32[]{:S(2)}, u32[]{:S(2)}) collective-permute-start(bf16[2,1,2,16,128]{4,3,2,1,0:T(8,128)(2,1)S(1)} %get-tuple-element.7), channel_id=1, source_target_pairs={{4,0},{8,4},{12,8},{16,12},{20,16},{24,20},{28,24},{5,1},{9,5},{13... | collective-permute-start | bytes 49160 | tf_op jit(solution)/shard_map/ppermute | solution.py:17
  19.5 2.6 %collective-permute-start.2 = (bf16[2,10,1,16,128]{4,3,2,1,0:T(8,128)(2,1)S(1)}, bf16[2,10,1,16,128]{4,3,2,1,0:T(8,128)(2,1)S(1)}, u32[]{:S(2)}, u32[]{:S(2)}) collective-permute-start(bf16[2,10,1,16,128]{4,3,2,1,0:T(8,128)(2,1)S(1)} %get-tuple-element.4), channel_id=1, source_target_pairs={{0,1},{1,2},{2,3},{4,5},{5,6},{6,7},{8,9},{9,10},{10,11},{12,13},{... | collective-permute-start | bytes 245768 | tf_op jit(solution)/shard_map/ppermute | solution.py:15
  20.8 4.9 %collective-permute-start.3 = (bf16[2,10,1,16,128]{4,3,2,1,0:T(8,128)(2,1)S(1)}, bf16[2,10,1,16,128]{4,3,2,1,0:T(8,128)(2,1)S(1)}, u32[]{:S(2)}, u32[]{:S(2)}) collective-permute-start(bf16[2,10,1,16,128]{4,3,2,1,0:T(8,128)(2,1)S(1)} %get-tuple-element.5), channel_id=1, source_target_pairs={{1,0},{2,1},{3,2},{5,4},{6,5},{7,6},{9,8},{10,9},{11,10},{13,12},{... | collective-permute-start | bytes 245768 | tf_op jit(solution)/shard_map/ppermute | solution.py:17
  31.3 6.4 %copy-start.4 = (bf16[8,2,16,128]{3,2,1,0:T(8,128)(2,1)S(1)}, bf16[8,2,16,128]{3,2,1,0:T(8,128)(2,1)}, u32[]{:S(2)}) copy-start(bf16[8,2,16,128]{3,2,1,0:T(8,128)(2,1)} %param.5) | copy-start | bytes 196612
  33.3 11.2 %all-to-all-start = ((bf16[4,2,2048]{2,1,0:T(2,128)(2,1)}), bf16[4,2,2048]{2,1,0:T(2,128)(2,1)S(1)}, u32[]{:S(2)}, u32[]{:S(2)}) async-start(bf16[4,2,2048]{2,1,0:T(2,128)(2,1)} %reshape.101), calls=%async_computation | async-start | bytes 65536 | tf_op jit(solution)/shard_map/all_to_all | solution.py:66
  37.7 76.6 %reduce-scatter.8.cloned.1.call-start = ((), (), s32[]{:S(2)}) async-start(), calls=%async_computation.5 | async-start | bytes 1990656 | tf_op jit(solution)/shard_map/reduce_scatter | solution.py:58
  43.2 1.3 copy-start.2
  44.5 91.3 %reduce-scatter.6.cloned.1.call-start = ((), (), s32[]{:S(2)}) async-start(), calls=%async_computation.4 | async-start | bytes 327680 | tf_op jit(solution)/shard_map/reduce_scatter | solution.py:71
  45.4 7.0 %collective-permute-start.4 = (bf16[4,1,8,128]{3,2,1,0:T(8,128)(2,1)S(1)}, bf16[4,1,8,128]{3,2,1,0:T(8,128)(2,1)S(1)}, u32[]{:S(2)}, u32[]{:S(2)}) collective-permute-start(bf16[4,1,8,128]{3,2,1,0:T(8,128)(2,1)S(1)} %get-tuple-element.8), channel_id=1, source_target_pairs={{0,4},{4,8},{8,12},{12,16},{16,20},{20,24},{24,28},{1,5},{5,9},{9,... | collective-permute-start | bytes 24584 | tf_op jit(solution)/shard_map/ppermute | solution.py:15
  49.7 13.6 %copy-start.1 = (bf16[3,3,3,512,128]{4,3,2,1,0:T(8,128)(2,1)S(1)}, bf16[3,3,3,512,128]{4,3,2,1,0:T(8,128)(2,1)}, u32[]{:S(2)}) copy-start(bf16[3,3,3,512,128]{4,3,2,1,0:T(8,128)(2,1)} %param.9) | copy-start | bytes 10616836
  49.7 5.8 %collective-permute-start.5 = (bf16[4,1,8,128]{3,2,1,0:T(8,128)(2,1)S(1)}, bf16[4,1,8,128]{3,2,1,0:T(8,128)(2,1)S(1)}, u32[]{:S(2)}, u32[]{:S(2)}) collective-permute-start(bf16[4,1,8,128]{3,2,1,0:T(8,128)(2,1)S(1)} %get-tuple-element.9), channel_id=1, source_target_pairs={{4,0},{8,4},{12,8},{16,12},{20,16},{24,20},{28,24},{5,1},{9,5},{13... | collective-permute-start | bytes 24584 | tf_op jit(solution)/shard_map/ppermute | solution.py:17
  67.9 90.4 %reduce-scatter.10.cloned.1.call-start = ((), (), s32[]{:S(2)}) async-start(), calls=%async_computation.6 | async-start | bytes 327680
Sparse Core Ops, SparseCore 0:
  44.6 69.6 reduce-scatter.7
  116.8 18.9 reduce-scatter.5
  138.2 20.0 reduce-scatter.9
where the time goes:
time: 168 us; the launch traced here: 167 us
  waiting for transfers between devices  95.8 us (57%)
  matrix products  23.3 us (14%)
  starting transfers between devices  19.1 us (11%)
  between operations  14.4 us (9%)
  local copies, waits for them, and re-layouts  9.76 us (6%)
  other arithmetic  4.41 us (3%)
    reduce_scatter x1, waiting for transfers between devices, body(): lax.psum_scatter(partial_taps, 'grp', scatter_dimension=3, tiled=True)  46.4 us
    unnamed x4, waiting for transfers between devices  21.2 us
    dot_general x54, matrix products, spread_taps(): jnp.einsum('xyzo,io->xyzi', window, kernel, preferred_element_type=jnp.fl...  17.5 us
    reduce_scatter x1, waiting for transfers between devices, body(): lax.psum_scatter(spread_taps(slab, filters_half, (count, coarse_extent[1]...  17.2 us
    ppermute x3, waiting for transfers between devices, padded_2(): lax.ppermute(head, axis, [((i + 1) % count, i) for i in range(ends)])  10.9 us
    ppermute x3, starting transfers between devices, padded_2(): lax.ppermute(tail, axis, [(i, (i + 1) % count) for i in range(ends)])  10.5 us
    unnamed x16, local copies, waits for them, and re-layouts  9.16 us
    dot_general x27, matrix products, body(): jnp.einsum('xyzi,xyzo->io', window, grad_out, preferred_element_type=jnp....  5.4 us
  transfers between devices with their start and end apart: 10, of which 7 were waited for; matrix products, arithmetic and copies ran while one was open for 15% of the time, Pallas kernels for 0%

commit v1 on v0

--- a/solution.py
+++ b/solution.py
@@ -63,7 +63,10 @@
     ).astype(jnp.bfloat16)
     coarse_extent = coarse.shape[:3]
     wide = filters_half.shape[3]
-    slab = lax.all_to_all(coarse, "chan", split_axis=3, concat_axis=0, tiled=True)
+    slab = jnp.concatenate(
+        lax.all_to_all(jnp.stack(jnp.split(coarse, lax.axis_size("chan"), axis=3)), "chan", 0, 0),
+        axis=0,
+    )
     slab = padded_2(slab, (("grp", 1),), 1)
     slab = jnp.pad(slab, ((1, 1), (0, 0), (1, 1), (0, 0)))
     count = lax.axis_size("chan") * coarse_extent[0]

time: 168 us -> 167 us (level)
  local copies, waits for them, and re-layouts: 9.76 us -> 7.51 us
    unnamed x16 -> x14, local copies, waits for them, and re-layouts: 9.16 us -> 7.43 us
where the time goes in v1:
time: 167 us; the launch traced here: 166 us
  waiting for transfers between devices  96.6 us (58%)
  matrix products  23.4 us (14%)
  starting transfers between devices  19.1 us (11%)
  between operations  14.4 us (9%)
  local copies, waits for them, and re-layouts  7.51 us (4%)
  other arithmetic  5.03 us (3%)
    reduce_scatter x1, waiting for transfers between devices, body(): lax.psum_scatter(partial_taps, 'grp', scatter_dimension=3, tiled=True)  47.1 us
    unnamed x4, waiting for transfers between devices  21.2 us
    dot_general x54, matrix products, spread_taps(): jnp.einsum('xyzo,io->xyzi', window, kernel, preferred_element_type=jnp.fl...  17.6 us
    reduce_scatter x1, waiting for transfers between devices, body(): lax.psum_scatter(spread_taps(slab, filters_half, (count, coarse_extent[1]...  17.2 us
    ppermute x3, waiting for transfers between devices, padded_2(): lax.ppermute(head, axis, [((i + 1) % count, i) for i in range(ends)])  10.9 us
    ppermute x3, starting transfers between devices, padded_2(): lax.ppermute(tail, axis, [(i, (i + 1) % count) for i in range(ends)])  10.5 us
    unnamed x14, local copies, waits for them, and re-layouts  7.43 us
    dot_general x27, matrix products, body(): jnp.einsum('xyzi,xyzo->io', window, grad_out, preferred_element_type=jnp....  5.4 us
  transfers between devices with their start and end apart: 10, of which 7 were waited for; matrix products, arithmetic and copies ran while one was open for 15% of the time, Pallas kernels for 0%

profile of v1, /device:TPU:0, one launch (start us, length us, event | category | flops | bytes accessed | tf_op | source)
XLA Modules:
  0.0 166.0 jit_solution(7691122758829953899)
XLA Ops:
  7.2 0.9 pad_maximum_fusion.3
  8.1 4.9 %collective-permute-start = (bf16[2,1,2,16,128]{4,3,2,1,0:T(8,128)(2,1)S(1)}, bf16[2,1,2,16,128]{4,3,2,1,0:T(8,128)(2,1)S(1)}, u32[]{:S(2)}, u32[]{:S(2)}) collective-permute-start(bf16[2,1,2,16,128]{4,3,2,1,0:T(8,128)(2,1)S(1)} %get-tuple-element.6), channel_id=1, source_target_pairs={{0,4},{4,8},{8,12},{12,16},{16,20},{20,24},{24,28},{1,5},{5,9},{9,... | collective-permute-start | bytes 49160 | tf_op jit(solution)/shard_map/ppermute | solution.py:15
  13.0 1.3 collective-permute-start.1
  14.4 4.2 %collective-permute-done.1 = bf16[2,1,2,16,128]{4,3,2,1,0:T(8,128)(2,1)S(1)} collective-permute-done((bf16[2,1,2,16,128]{4,3,2,1,0:T(8,128)(2,1)S(1)}, bf16[2,1,2,16,128]{4,3,2,1,0:T(8,128)(2,1)S(1)}, u32[]{:S(2)}, u32[]{:S(2)}) %collective-permute-start.1) | collective-permute-done | bytes 16416 | tf_op jit(solution)/shard_map/ppermute | solution.py:17
  18.6 0.9 pad_maximum_fusion
  19.5 1.3 collective-permute-start.2
  20.8 1.3 collective-permute-start.3
  22.1 3.6 %collective-permute-done.3 = bf16[2,10,1,16,128]{4,3,2,1,0:T(8,128)(2,1)S(1)} collective-permute-done((bf16[2,10,1,16,128]{4,3,2,1,0:T(8,128)(2,1)S(1)}, bf16[2,10,1,16,128]{4,3,2,1,0:T(8,128)(2,1)S(1)}, u32[]{:S(2)}, u32[]{:S(2)}) %collective-permute-start.3) | collective-permute-done | bytes 81952 | tf_op jit(solution)/shard_map/ppermute | solution.py:17
  25.7 1.1 select_maximum_fusion
  31.9 0.6 pad_maximum_fusion.1
  32.6 4.4 %all-to-all-start = ((bf16[4,1,4,8,128]{4,3,2,1,0:T(8,128)(2,1)}), bf16[4,1,4,8,128]{4,3,2,1,0:T(8,128)(2,1)S(1)}, u32[]{:S(2)}, u32[]{:S(2)}) async-start(bf16[4,1,4,8,128]{4,3,2,1,0:T(8,128)(2,1)} %pad_maximum_fusion.1), calls=%async_computation | async-start | bytes 65536 | tf_op jit(solution)/shard_map/all_to_all | solution.py:67
  42.4 1.2 copy-done.2
  43.7 4.3 %collective-permute-start.4 = (bf16[4,1,8,128]{3,2,1,0:T(8,128)(2,1)S(1)}, bf16[4,1,8,128]{3,2,1,0:T(8,128)(2,1)S(1)}, u32[]{:S(2)}, u32[]{:S(2)}) collective-permute-start(bf16[4,1,8,128]{3,2,1,0:T(8,128)(2,1)S(1)} %get-tuple-element.8), channel_id=1, source_target_pairs={{0,4},{4,8},{8,12},{12,16},{16,20},{20,24},{24,28},{1,5},{5,9},{9,... | collective-permute-start | bytes 24584 | tf_op jit(solution)/shard_map/ppermute | solution.py:15
  48.1 1.6 collective-permute-start.5
  49.7 1.1 fusion.71
  50.8 3.1 %collective-permute-done.5 = bf16[4,1,8,128]{3,2,1,0:T(8,128)(2,1)S(1)} collective-permute-done((bf16[4,1,8,128]{3,2,1,0:T(8,128)(2,1)S(1)}, bf16[4,1,8,128]{3,2,1,0:T(8,128)(2,1)S(1)}, u32[]{:S(2)}, u32[]{:S(2)}) %collective-permute-start.5) | collective-permute-done | bytes 8224 | tf_op jit(solution)/shard_map/ppermute | solution.py:17
  54.0 1.1 fusion.59
  55.1 1.1 fusion.61
  56.2 1.1 fusion.63
  57.3 1.1 fusion.65
  58.4 1.1 fusion.69
  59.5 1.1 fusion.73
  60.6 1.1 fusion.87
  65.3 0.9 convolution_add_fusion.2
  66.3 47.1 %reduce-scatter.8.cloned.1.call-done = f32[3,3,3,16,128]{4,3,2,1,0:T(8,128)} async-done(((f32[3,3,3,128,128]{4,3,2,1,0:T(8,128)}), f32[3,3,3,16,128]{4,3,2,1,0:T(8,128)}) %reduce-scatter.8.cloned.1.call-update) | async-done | bytes 221200 | tf_op jit(solution)/shard_map/reduce_scatter | solution.py:58
  113.4 2.5 %copy.91 = f32[3,3,3,16,128]{3,2,1,0,4:T(4,128)S(1)} copy(f32[3,3,3,16,128]{4,3,2,1,0:T(8,128)} %reduce-scatter.8.cloned.1.call-done) | data formatting | bytes 442368
  115.9 1.7 %reshape.103 = f32[128,432]{1,0:T(8,128)} reshape(f32[128,3,3,3,16]{4,3,2,1,0:T(4,128)S(1)} %bitcast.659) | data formatting | bytes 442368
  117.6 17.2 %reduce-scatter.6.cloned.1.call-done = f32[1,4,8,512]{3,2,1,0:T(8,128)} async-done(((f32[4,4,8,512]{3,2,1,0:T(8,128)}), f32[1,4,8,512]{3,2,1,0:T(8,128)}) %reduce-scatter.6.cloned.1.call-update) | async-done | bytes 65552 | tf_op jit(solution)/shard_map/reduce_scatter | solution.py:74
  134.9 1.5 convert_element_type.27
  136.3 21.1 %reduce-scatter.10.cloned.1.call-done = f32[32,432]{1,0:T(8,128)} async-done(((f32[128,432]{1,0:T(8,128)}), f32[32,432]{1,0:T(8,128)}) %reduce-scatter.10.cloned.1.call-update) | async-done | bytes 55312
  157.4 1.1 reshape.104
  158.6 0.9 copy.92
  (97 shorter events, 14.1 us)
Async XLA Ops:
  7.2 24.3 %copy-start = (bf16[2,2,2,512,128]{4,3,2,1,0:T(8,128)(2,1)S(1)}, bf16[2,2,2,512,128]{4,3,2,1,0:T(8,128)(2,1)}, u32[]{:S(2)}) copy-start(bf16[2,2,2,512,128]{4,3,2,1,0:T(8,128)(2,1)} %param.8) | copy-start | bytes 3145732
  7.2 19.7 %copy-start.3 = (bf16[3,3,3,128,128]{4,3,2,1,0:T(8,128)(2,1)S(1)}, bf16[3,3,3,128,128]{4,3,2,1,0:T(8,128)(2,1)}, u32[]{:S(2)}) copy-start(bf16[3,3,3,128,128]{4,3,2,1,0:T(8,128)(2,1)} %param.7) | copy-start | bytes 2654212
  8.1 6.3 %collective-permute-start = (bf16[2,1,2,16,128]{4,3,2,1,0:T(8,128)(2,1)S(1)}, bf16[2,1,2,16,128]{4,3,2,1,0:T(8,128)(2,1)S(1)}, u32[]{:S(2)}, u32[]{:S(2)}) collective-permute-start(bf16[2,1,2,16,128]{4,3,2,1,0:T(8,128)(2,1)S(1)} %get-tuple-element.6), channel_id=1, source_target_pairs={{0,4},{4,8},{8,12},{12,16},{16,20},{20,24},{24,28},{1,5},{5,9},{9,... | collective-permute-start | bytes 49160 | tf_op jit(solution)/shard_map/ppermute | solution.py:15
  13.0 5.6 %collective-permute-start.1 = (bf16[2,1,2,16,128]{4,3,2,1,0:T(8,128)(2,1)S(1)}, bf16[2,1,2,16,128]{4,3,2,1,0:T(8,128)(2,1)S(1)}, u32[]{:S(2)}, u32[]{:S(2)}) collective-permute-start(bf16[2,1,2,16,128]{4,3,2,1,0:T(8,128)(2,1)S(1)} %get-tuple-element.7), channel_id=1, source_target_pairs={{4,0},{8,4},{12,8},{16,12},{20,16},{24,20},{28,24},{5,1},{9,5},{13... | collective-permute-start | bytes 49160 | tf_op jit(solution)/shard_map/ppermute | solution.py:17
  19.5 2.6 %collective-permute-start.2 = (bf16[2,10,1,16,128]{4,3,2,1,0:T(8,128)(2,1)S(1)}, bf16[2,10,1,16,128]{4,3,2,1,0:T(8,128)(2,1)S(1)}, u32[]{:S(2)}, u32[]{:S(2)}) collective-permute-start(bf16[2,10,1,16,128]{4,3,2,1,0:T(8,128)(2,1)S(1)} %get-tuple-element.4), channel_id=1, source_target_pairs={{0,1},{1,2},{2,3},{4,5},{5,6},{6,7},{8,9},{9,10},{10,11},{12,13},{... | collective-permute-start | bytes 245768 | tf_op jit(solution)/shard_map/ppermute | solution.py:15
  20.8 4.9 %collective-permute-start.3 = (bf16[2,10,1,16,128]{4,3,2,1,0:T(8,128)(2,1)S(1)}, bf16[2,10,1,16,128]{4,3,2,1,0:T(8,128)(2,1)S(1)}, u32[]{:S(2)}, u32[]{:S(2)}) collective-permute-start(bf16[2,10,1,16,128]{4,3,2,1,0:T(8,128)(2,1)S(1)} %get-tuple-element.5), channel_id=1, source_target_pairs={{1,0},{2,1},{3,2},{5,4},{6,5},{7,6},{9,8},{10,9},{11,10},{13,12},{... | collective-permute-start | bytes 245768 | tf_op jit(solution)/shard_map/ppermute | solution.py:17
  30.8 6.1 %copy-start.4 = (bf16[8,2,16,128]{3,2,1,0:T(8,128)(2,1)S(1)}, bf16[8,2,16,128]{3,2,1,0:T(8,128)(2,1)}, u32[]{:S(2)}) copy-start(bf16[8,2,16,128]{3,2,1,0:T(8,128)(2,1)} %param.5) | copy-start | bytes 196612
  32.6 11.2 %all-to-all-start = ((bf16[4,1,4,8,128]{4,3,2,1,0:T(8,128)(2,1)}), bf16[4,1,4,8,128]{4,3,2,1,0:T(8,128)(2,1)S(1)}, u32[]{:S(2)}, u32[]{:S(2)}) async-start(bf16[4,1,4,8,128]{4,3,2,1,0:T(8,128)(2,1)} %pad_maximum_fusion.1), calls=%async_computation | async-start | bytes 65536 | tf_op jit(solution)/shard_map/all_to_all | solution.py:67
  36.9 76.5 %reduce-scatter.8.cloned.1.call-start = ((), (), s32[]{:S(2)}) async-start(), calls=%async_computation.5 | async-start | bytes 1990656 | tf_op jit(solution)/shard_map/reduce_scatter | solution.py:58
  42.4 1.2 copy-start.2
  43.7 91.2 %reduce-scatter.6.cloned.1.call-start = ((), (), s32[]{:S(2)}) async-start(), calls=%async_computation.4 | async-start | bytes 327680 | tf_op jit(solution)/shard_map/reduce_scatter | solution.py:74
  43.7 7.0 %collective-permute-start.4 = (bf16[4,1,8,128]{3,2,1,0:T(8,128)(2,1)S(1)}, bf16[4,1,8,128]{3,2,1,0:T(8,128)(2,1)S(1)}, u32[]{:S(2)}, u32[]{:S(2)}) collective-permute-start(bf16[4,1,8,128]{3,2,1,0:T(8,128)(2,1)S(1)} %get-tuple-element.8), channel_id=1, source_target_pairs={{0,4},{4,8},{8,12},{12,16},{16,20},{20,24},{24,28},{1,5},{5,9},{9,... | collective-permute-start | bytes 24584 | tf_op jit(solution)/shard_map/ppermute | solution.py:15
  48.1 13.6 %copy-start.1 = (bf16[3,3,3,512,128]{4,3,2,1,0:T(8,128)(2,1)S(1)}, bf16[3,3,3,512,128]{4,3,2,1,0:T(8,128)(2,1)}, u32[]{:S(2)}) copy-start(bf16[3,3,3,512,128]{4,3,2,1,0:T(8,128)(2,1)} %param.9) | copy-start | bytes 10616836
  48.1 5.8 %collective-permute-start.5 = (bf16[4,1,8,128]{3,2,1,0:T(8,128)(2,1)S(1)}, bf16[4,1,8,128]{3,2,1,0:T(8,128)(2,1)S(1)}, u32[]{:S(2)}, u32[]{:S(2)}) collective-permute-start(bf16[4,1,8,128]{3,2,1,0:T(8,128)(2,1)S(1)} %get-tuple-element.9), channel_id=1, source_target_pairs={{4,0},{8,4},{12,8},{16,12},{20,16},{24,20},{28,24},{5,1},{9,5},{13... | collective-permute-start | bytes 24584 | tf_op jit(solution)/shard_map/ppermute | solution.py:17
  66.2 91.2 %reduce-scatter.10.cloned.1.call-start = ((), (), s32[]{:S(2)}) async-start(), calls=%async_computation.6 | async-start | bytes 327680
Sparse Core Ops, SparseCore 0:
  43.8 69.5 reduce-scatter.7
  115.9 18.9 reduce-scatter.5
  137.3 20.0 reduce-scatter.9
